TPU v7x, 128 devices: a whole 4x4x4 slice. The times are simulated.
128 devices in a mesh: fsdp: 8 (over x, z_hi), tensor: 16 (over z_lo, y, core).
Axes of the slice: x: 4, y: 4, z: 4 (z_hi: 2, z_lo: 2; z = z_hi * 2 + z_lo), core: 2. Of those that a mesh axis runs over, the one named last changes fastest.
Arguments:
- tokens: bfloat16 [3072, 8192], P(('fsdp', 'tensor')), may hold values from -6 to 6
- out_grad: bfloat16 [3072, 8192], P(('fsdp', 'tensor')), may hold values from -6 to 6
- up_weight: bfloat16 [256, 8, 128, 128], P('tensor', 'fsdp'), may hold values from -0.1875 to 0.1875
- down_weight: bfloat16 [256, 8, 128, 128], P('tensor', 'fsdp'), may hold values from -0.09375 to 0.09375
- up_index: int32 [256, 8], P('tensor'), may hold values from 0 to 63, all different within a row
- down_index: int32 [256, 8], P('tensor'), may hold values from 0 to 63, all different within a row
Outputs:
- mixed: bfloat16 [3072, 8192], P(('fsdp', 'tensor'))
- input_grad: bfloat16 [3072, 8192], P(('fsdp', 'tensor'))
- up_grad: float32 [256, 8, 128, 128], P('tensor', 'fsdp')
- down_grad: float32 [256, 8, 128, 128], P('tensor', 'fsdp')
Inputs may be any that keep to these rules, and one draw needn't show every extreme that they name: Each row of up_index names 8 different input blocks; every block is named somewhere. Each row of down_index names 8 different output blocks; every block is named somewhere.
All inputs are finite; a program needn't handle non-finite values.
Results may differ from a plain program's by a relative error of at most 0.024.
Values may be sent and summed in bfloat16 or wider, within the bound.
A program may use at most 192 MiB of HBM per device.

v0:
```python
import jax
import jax.numpy as jnp
from jax import lax
from jax.sharding import PartitionSpec as P

BLK = 128


def expand(row_block, block_index):
    blocks = row_block.reshape(row_block.shape[0], row_block.shape[1] // BLK, BLK)
    return jnp.take(blocks, block_index, axis=1)


def up_product(chosen, tiles):
    return jnp.einsum("rjki,jkio->rjo", chosen, tiles, preferred_element_type=jnp.float32)


def block_sum(slot_terms, block_index, block_count):
    row_count = slot_terms.shape[0]
    columns = lax.broadcasted_iota(jnp.int32, (1, 1, block_count), 2)
    selector = (block_index[:, :, None] == columns).astype(jnp.bfloat16)
    upper = slot_terms.astype(jnp.bfloat16)
    lower = (slot_terms - upper.astype(jnp.float32)).astype(jnp.bfloat16)
    total = jnp.einsum("rjko,jkb->rbo", upper, selector, preferred_element_type=jnp.float32)
    total = total + jnp.einsum("rjko,jkb->rbo", lower, selector, preferred_element_type=jnp.float32)
    return total.reshape(row_count, block_count * BLK)


def body(tokens, out_grad, up_weight, down_weight, up_index, down_index):
    row_block = lax.all_gather(tokens, "tensor", axis=0, tiled=True)
    block_count = row_block.shape[1] // BLK
    chosen = expand(row_block, up_index)
    preact = up_product(chosen, lax.all_gather(up_weight, "fsdp", axis=1, tiled=True))
    hidden = jax.nn.silu(preact).astype(jnp.bfloat16)
    down_full = lax.all_gather(down_weight, "fsdp", axis=1, tiled=True)
    slot_terms = jnp.einsum("rji,jkio->rjko", hidden, down_full, preferred_element_type=jnp.float32)
    mixed_rows = lax.psum_scatter(
        block_sum(slot_terms, down_index, block_count).astype(jnp.bfloat16),
        "tensor",
        scatter_dimension=0,
        tiled=True,
    )
    grad_rows = lax.all_gather(out_grad, "tensor", axis=0, tiled=True)
    picked = expand(grad_rows, down_index)
    up_full = lax.all_gather(up_weight, "fsdp", axis=1, tiled=True)
    hidden_grad = jnp.einsum(
        "rjko,jkio->rji", picked, down_full, preferred_element_type=jnp.float32
    )
    gate_sigma = jax.nn.sigmoid(preact)
    pre_grad = (hidden_grad * gate_sigma * (1.0 + preact * (1.0 - gate_sigma))).astype(jnp.bfloat16)
    down_terms = jnp.einsum("rji,rjko->jkio", hidden, picked, preferred_element_type=jnp.float32)
    down_grad = lax.psum_scatter(
        down_terms.astype(jnp.bfloat16), "fsdp", scatter_dimension=1, tiled=True
    ).astype(jnp.float32)
    up_terms = jnp.einsum("rjki,rjo->jkio", chosen, pre_grad, preferred_element_type=jnp.float32)
    up_grad = lax.psum_scatter(
        up_terms.astype(jnp.bfloat16), "fsdp", scatter_dimension=1, tiled=True
    ).astype(jnp.float32)
    slot_terms = jnp.einsum("rjo,jkio->rjki", pre_grad, up_full, preferred_element_type=jnp.float32)
    input_rows = lax.psum_scatter(
        block_sum(slot_terms, up_index, block_count).astype(jnp.bfloat16),
        "tensor",
        scatter_dimension=0,
        tiled=True,
    )
    return (mixed_rows, input_rows, up_grad, down_grad)


def solution(mesh):
    return jax.shard_map(
        body,
        mesh=mesh,
        in_specs=(
            P(("fsdp", "tensor"), None),
            P(("fsdp", "tensor"), None),
            P("tensor", "fsdp", None, None),
            P("tensor", "fsdp", None, None),
            P("tensor", None),
            P("tensor", None),
        ),
        out_specs=(
            P(("fsdp", "tensor"), None),
            P(("fsdp", "tensor"), None),
            P("tensor", "fsdp", None, None),
            P("tensor", "fsdp", None, None),
        ),
        check_vma=False,
    )
```

profile of v0, /device:TPU:0, one launch (start us, length us, event | category | flops | bytes accessed | tf_op | source)
XLA Modules:
  0.0 775.7 jit_solution(3806527784943739303)
XLA Ops:
  7.9 0.7 all-gather.11.cloned.1.call-update
  13.3 41.3 %all-gather.5.cloned.1.call-done = bf16[384,8192]{1,0:T(8,128)(2,1)} async-done(((bf16[24,8192]{1,0:T(8,128)(2,1)}), bf16[384,8192]{1,0:T(8,128)(2,1)}) %all-gather.5.cloned.1.call-update) | async-done | bytes 6291472 | tf_op jit(solution)/shard_map/all_gather | solution.py:30
  54.6 8.6 %copy.54 = bf16[384,8192]{0,1:T(8,128)(2,1)} copy(bf16[384,8192]{1,0:T(8,128)(2,1)} %all-gather.5.cloned.1.call-done) | data formatting | bytes 12582912 | tf_op jit(solution)/shard_map/all_gather | solution.py:30
  63.2 8.4 %copy.56 = bf16[384,64,128]{2,0,1:T(8,128)(2,1)} copy(bf16[384,64,128]{0,2,1:T(8,128)(2,1)} %bitcast.149) | data formatting | bytes 12582912 | tf_op jit(solution)/shard_map/reshape | solution.py:10
  71.6 27.9 %all-gather.11.cloned.1.call-done = bf16[384,8192]{1,0:T(8,128)(2,1)} async-done(((bf16[24,8192]{1,0:T(8,128)(2,1)}), bf16[384,8192]{1,0:T(8,128)(2,1)}) %all-gather.11.cloned.1.call-update) | async-done | bytes 6291472 | tf_op jit(solution)/shard_map/all_gather | solution.py:43
  99.5 8.6 %copy.62 = bf16[384,8192]{0,1:T(8,128)(2,1)} copy(bf16[384,8192]{1,0:T(8,128)(2,1)} %all-gather.11.cloned.1.call-done) | data formatting | bytes 12582912 | tf_op jit(solution)/shard_map/all_gather | solution.py:43
  108.1 8.7 %copy.64 = bf16[384,64,128]{2,0,1:T(8,128)(2,1)} copy(bf16[384,64,128]{0,2,1:T(8,128)(2,1)} %bitcast.150) | data formatting | bytes 12582912 | tf_op jit(solution)/shard_map/reshape | solution.py:10
  116.8 11.2 %gather_fusion.1 = bf16[128,384,128]{2,1,0:T(8,128)(2,1)} fusion(bf16[384,64,128]{2,0,1:T(8,128)(2,1)} %copy.64, s32[1024]{0:T(1024)S(1)} %pad_clamp_fusion), kind=kCustom, calls=%fused_computation.1.clone | custom fusion | bytes 25166336 | tf_op jit(solution)/shard_map/jit(_take)/gather | solution.py:11
  128.0 16.2 %copy.65 = bf16[16,8,384,128]{2,3,1,0:T(8,128)(2,1)} copy(bf16[16,8,384,128]{3,2,1,0:T(8,128)(2,1)} %bitcast.145) | data formatting | bytes 25165824 | tf_op jit(solution)/shard_map/jit(_take)/gather | solution.py:11
  144.2 11.3 %gather_fusion = bf16[128,384,128]{2,1,0:T(8,128)(2,1)} fusion(bf16[384,64,128]{2,0,1:T(8,128)(2,1)} %copy.56, s32[1024]{0:T(1024)S(1)} %pad_clamp_fusion.1), kind=kCustom, calls=%fused_computation.clone | custom fusion | bytes 25166336 | tf_op jit(solution)/shard_map/jit(_take)/gather | solution.py:11
  155.5 16.2 %copy.57 = bf16[16,8,384,128]{2,3,1,0:T(8,128)(2,1)} copy(bf16[16,8,384,128]{3,2,1,0:T(8,128)(2,1)} %bitcast.146) | data formatting | bytes 25165824 | tf_op jit(solution)/shard_map/jit(_take)/gather | solution.py:11
  171.7 2.4 all-gather.7.cloned.1.call-done
  174.1 9.8 %fusion.10 = f32[16,384,128,1]{2,1,3,0:T(8,128)S(1)} fusion(bf16[16,8,128,128]{3,2,1,0:T(8,128)(2,1)} %all-gather.7.cloned.1.call-done, bf16[16,8,384,128]{2,3,1,0:T(8,128)(2,1)} %copy.57, pred[16,8]{1,0:T(8,128)(4,1)S(1)} %copy.53), kind=kOutput, calls=%fused_computation.18 | convolution fusion | flops 1616904192 | bytes 19923072 | tf_op jit(solution)/shard_map/rjki,jkio->rjo/dot_general | solution.py:15
  183.9 10.3 %convert_bitcast_fusion = bf16[16,8,128,128]{2,3,1,0:T(8,128)(2,1)} fusion(bf16[16,8,384,128]{2,3,1,0:T(8,128)(2,1)} %copy.65, pred[16,8]{1,0:T(8,128)(4,1)S(1)} %copy.61, f32[16,384,128,1]{2,1,3,0:T(8,128)S(1)} %fusion.10), kind=kOutput, calls=%fused_computation.36 | convolution fusion | flops 1622933504 | bytes 19923072 | tf_op jit(solution)/shard_map/rji,rjko->jkio/dot_general | solution.py:51
  194.2 51.4 %all-gather.9.cloned.1.call-done = bf16[16,8,128,128]{3,2,1,0:T(8,128)(2,1)} async-done(((bf16[16,1,128,128]{3,2,1,0:T(8,128)(2,1)}), bf16[16,8,128,128]{3,2,1,0:T(8,128)(2,1)}) %all-gather.9.cloned.1.call-update) | async-done | bytes 4194320 | tf_op jit(solution)/shard_map/all_gather | solution.py:35
  245.6 21.3 %fusion.29 = bf16[384,16,128]{2,0,1:T(8,128)(2,1)} fusion(f32[16,384,128,1]{2,1,3,0:T(8,128)S(1)} %fusion.10, bf16[16,8,128,128]{3,2,1,0:T(8,128)(2,1)} %all-gather.9.cloned.1.call-done, bf16[16,8,384,128]{2,3,1,0:T(8,128)(2,1)} %copy.65, pred[16,8]{1,0:T(8,128)(4,1)S(1)} %copy.61), kind=kOutput, calls=%fused_computation.39 | convolution fusion | flops 1623982080 | bytes 21495936 | tf_op jit(solution)/shard_map/rjko,jkio->rji/dot_general | solution.py:46
  266.9 10.5 %fusion.35 = bf16[16,8,128,128]{3,2,1,0:T(8,128)(2,1)} fusion(bf16[16,8,384,128]{2,3,1,0:T(8,128)(2,1)} %copy.57, pred[16,8]{1,0:T(8,128)(4,1)S(1)} %copy.53, bf16[384,16,128]{2,0,1:T(8,128)(2,1)} %fusion.29), kind=kOutput, calls=%fused_computation.48 | convolution fusion | flops 1619001344 | bytes 18350208 | tf_op jit(solution)/shard_map/rjki,rjo->jkio/dot_general | solution.py:55
  277.5 12.9 %fusion.1 = (bf16[384,16,8,128]{3,0,2,1:T(8,128)(2,1)}, bf16[384,16,8,128]{3,0,2,1:T(8,128)(2,1)}) fusion(bf16[16,8,128,128]{3,2,1,0:T(8,128)(2,1)} %all-gather.9.cloned.1.call-done, f32[16,384,128,1]{2,1,3,0:T(8,128)S(1)} %fusion.10), kind=kOutput, calls=%fused_computation.7 | convolution fusion | flops 1639710720 | bytes 32505856 | tf_op jit(solution)/shard_map/rji,jkio->rjko/dot_general | solution.py:36
  290.4 17.5 %fusion.16 = f32[64,384,128,1]{2,0,3,1:T(8,128)} fusion(bf16[384,16,8,128]{3,0,2,1:T(8,128)(2,1)} %get-tuple-element.25, s32[16,8]{0,1:T(8,128)S(1)} %copy-done.1), kind=kOutput, calls=%fused_computation.24 | convolution fusion | flops 805314560 | bytes 25166336 | tf_op jit(solution)/shard_map/rjko,jkb->rbo/dot_general | solution.py:25
  307.9 20.4 %fusion.7 = bf16[64,384,128]{2,0,1:T(8,128)(2,1)} fusion(f32[64,384,128,1]{2,0,3,1:T(8,128)} %fusion.16, bf16[384,16,8,128]{3,0,2,1:T(8,128)(2,1)} %get-tuple-element.26, s32[16,8]{0,1:T(8,128)S(1)} %copy-done.1), kind=kOutput, calls=%fused_computation.15 | convolution fusion | flops 811606016 | bytes 31457792 | tf_op jit(solution)/shard_map/rjko,jkb->rbo/dot_general | solution.py:24
  328.3 18.1 %copy.101 = bf16[48,8,64,128]{3,1,2,0:T(8,128)(2,1)} copy(bf16[48,8,64,128]{3,2,1,0:T(8,128)(2,1)} %bitcast.151) | data formatting | bytes 12582912
  346.5 1.3 copy-done
  347.8 13.1 %fusion = (bf16[384,16,8,128]{3,0,2,1:T(8,128)(2,1)}, bf16[384,16,8,128]{3,0,2,1:T(8,128)(2,1)}) fusion(bf16[16,8,128,128]{3,2,1,0:T(8,128)(2,1)} %all-gather.7.cloned.1.call-done, bf16[384,16,128]{2,0,1:T(8,128)(2,1)S(1)} %copy-done), kind=kOutput, calls=%fused_computation.4 | convolution fusion | flops 1635778560 | bytes 30932992 | tf_op jit(solution)/shard_map/rjo,jkio->rjki/dot_general | solution.py:59
  360.8 17.6 %fusion.12 = f32[64,384,128,1]{2,0,3,1:T(8,128)} fusion(bf16[384,16,8,128]{3,0,2,1:T(8,128)(2,1)} %get-tuple-element.23, s32[16,8]{0,1:T(8,128)S(1)} %copy-done.2), kind=kOutput, calls=%fused_computation.20 | convolution fusion | flops 805314560 | bytes 25166336 | tf_op jit(solution)/shard_map/rjko,jkb->rbo/dot_general | solution.py:25
  378.4 20.5 %fusion.2 = bf16[64,384,128]{2,0,1:T(8,128)(2,1)} fusion(f32[64,384,128,1]{2,0,3,1:T(8,128)} %fusion.12, bf16[384,16,8,128]{3,0,2,1:T(8,128)(2,1)} %get-tuple-element.24, s32[16,8]{0,1:T(8,128)S(1)} %copy-done.2), kind=kOutput, calls=%fused_computation.9 | convolution fusion | flops 811606016 | bytes 31457792 | tf_op jit(solution)/shard_map/rjko,jkb->rbo/dot_general | solution.py:24
  398.9 18.1 %copy.100 = bf16[48,8,64,128]{3,1,2,0:T(8,128)(2,1)} copy(bf16[48,8,64,128]{3,2,1,0:T(8,128)(2,1)} %bitcast.152) | data formatting | bytes 12582912
  418.3 199.9 %all-reduce.5.cloned.1.call-done = (bf16[16,8,128,128]{3,2,1,0:T(8,128)(2,1)}, bf16[16,8,128,128]{2,3,1,0:T(8,128)(2,1)}) async-done(((bf16[16,8,128,128]{3,2,1,0:T(8,128)(2,1)}, bf16[16,8,128,128]{2,3,1,0:T(8,128)(2,1)}), (bf16[16,8,128,128]{3,2,1,0:T(8,128)(2,1)}, bf16[16,8,128,128]{2,3,1,0:T(8,128)(2,1)})) %all-reduce.5.cloned.1.call-update) | async-done | bytes 8388624
  618.2 1.8 dynamic-slice_convert_fusion
  620.0 1.3 copy.69
  621.3 2.8 dynamic-slice_convert_fusion.1
  624.1 72.2 %reduce-scatter.9.cloned.1.call-done = bf16[24,8192]{1,0:T(8,128)(2,1)} async-done(((bf16[384,8192]{1,0:T(8,128)(2,1)}), bf16[24,8192]{1,0:T(8,128)(2,1)}) %reduce-scatter.9.cloned.1.call-update) | async-done | bytes 393232 | tf_op jit(solution)/shard_map/reduce_scatter | solution.py:37
  696.3 72.4 %reduce-scatter.11.cloned.1.call-done = bf16[24,8192]{1,0:T(8,128)(2,1)} async-done(((bf16[384,8192]{1,0:T(8,128)(2,1)}), bf16[24,8192]{1,0:T(8,128)(2,1)}) %reduce-scatter.11.cloned.1.call-update) | async-done | bytes 393232 | tf_op jit(solution)/shard_map/reduce_scatter | solution.py:60
  (33 shorter events, 6.8 us)
Async XLA Ops:
  7.2 47.4 %all-gather.5.cloned.1.call-start = ((), (), s32[]{:S(2)}) async-start(), calls=%async_computation.2 | async-start | bytes 6684672 | tf_op jit(solution)/shard_map/all_gather | solution.py:30
  7.9 91.6 %all-gather.11.cloned.1.call-start = ((), (), s32[]{:S(2)}) async-start(), calls=%async_computation.6 | async-start | bytes 6684672 | tf_op jit(solution)/shard_map/all_gather | solution.py:43
  8.6 165.5 %all-gather.7.cloned.1.call-start = ((), (), s32[]{:S(2)}) async-start(), calls=%async_computation.3 | async-start | bytes 4718592 | tf_op jit(solution)/shard_map/all_gather | solution.py:33
  9.4 236.3 %all-gather.9.cloned.1.call-start = ((), (), s32[]{:S(2)}) async-start(), calls=%async_computation.4 | async-start | bytes 4718592 | tf_op jit(solution)/shard_map/all_gather | solution.py:35
  10.0 608.2 %all-reduce.5.cloned.1.call-start = ((), (), s32[]{:S(2)}) async-start(), calls=%async_computation.8 | async-start | bytes 16777216
  277.5 12.9 %copy-start.1 = (s32[16,8]{0,1:T(8,128)S(1)}, s32[16,8]{0,1:T(8,128)}, u32[]{:S(2)}) copy-start(s32[16,8]{0,1:T(8,128)} %param.13) | copy-start | bytes 1540
  277.5 418.8 %reduce-scatter.9.cloned.1.call-start = ((), (), s32[]{:S(2)}) async-start(), calls=%async_computation.5 | async-start | bytes 6684672 | tf_op jit(solution)/shard_map/reduce_scatter | solution.py:37
  346.4 1.4 copy-start
  346.4 14.4 %copy-start.2 = (s32[16,8]{0,1:T(8,128)S(1)}, s32[16,8]{0,1:T(8,128)}, u32[]{:S(2)}) copy-start(s32[16,8]{0,1:T(8,128)} %param.12) | copy-start | bytes 1540
  346.4 422.2 %reduce-scatter.11.cloned.1.call-start = ((), (), s32[]{:S(2)}) async-start(), calls=%async_computation.7 | async-start | bytes 6684672 | tf_op jit(solution)/shard_map/reduce_scatter | solution.py:60
  417.0 0.7 copy-start.3
Sparse Core Ops, SparseCore 0:
  9.7 44.8 all-gather.4
  56.3 43.1 all-gather.10
  101.8 72.2 all-gather.6
  176.3 69.2 all-gather.8
  277.6 340.5 all-reduce.4
  621.0 75.2 reduce-scatter.8
  699.2 69.3 reduce-scatter.10
where the time goes:
time: 777 us; the launch traced here: 776 us
  waiting for transfers between devices  470 us (60%)
  matrix products  154 us (20%)
  local copies, waits for them, and re-layouts  130 us (17%)
  between operations  14.4 us (2%)
    unnamed x8, waiting for transfers between devices  202 us
    reduce_scatter x1, waiting for transfers between devices, body(): lax.psum_scatter(block_sum(slot_terms, up_index, block_count).astype(jnp....  72.4 us
    reduce_scatter x1, waiting for transfers between devices, body(): lax.psum_scatter(block_sum(slot_terms, down_index, block_count).astype(jn...  72.2 us
    gather x4, local copies, waits for them, and re-layouts, expand(): return jnp.take(blocks, block_index, axis=1)  54.9 us
    all_gather x1, waiting for transfers between devices, body(): down_full = lax.all_gather(down_weight, 'fsdp', axis=1, tiled=True)  51.4 us
    all_gather x1, waiting for transfers between devices, body(): row_block = lax.all_gather(tokens, 'tensor', axis=0, tiled=True)  41.3 us
    dot_general x2, matrix products, block_sum(): jnp.einsum('rjko,jkb->rbo', upper, selector, preferred_element_type=jnp.f...  40.9 us
    unnamed x12, local copies, waits for them, and re-layouts  40.1 us
  transfers between devices with their start and end apart: 7, of which 7 were waited for; matrix products, arithmetic and copies ran while one was open for 33% of the time, Pallas kernels for 0%

commit v1 on v0

v1 whole, which is shorter than its diff:
```python
import functools

import jax
import jax.numpy as jnp
from jax import lax
from jax.experimental import pallas as pl
from jax.experimental.pallas import tpu as pltpu
from jax.sharding import PartitionSpec as P

MESH = pl.DeviceIdType.MESH
F32, BF = jnp.float32, jnp.bfloat16
BLK = 128


def place():
    f = lax.axis_index("fsdp"); t = lax.axis_index("tensor")
    return f // 2, f % 2, (t // 2) % 4, t // 8, t % 2

def fdev(x, zh): return x * 2 + zh
def tdev(y, zl, c): return (zl * 4 + y) * 2 + c

def gather_kernel(do_f, do_t, do_e, tok, og, upw, dww, tok_o, og_o, up_o, dw_o, ss, rs, ls):
    x, zh, y, zl, c = place()
    f, t = fdev(x, zh), tdev(y, zl, c)
    xp, xm = (x + 1) % 4, (x + 3) % 4
    yp, ym = (y + 1) % 4, (y + 3) % 4
    FP, FM, FZ = (fdev(xp, zh), t), (fdev(xm, zh), t), (fdev(x, 1 - zh), t)
    TP, TM, TZ, TC = (f, tdev(yp, zl, c)), (f, tdev(ym, zl, c)), (f, tdev(y, 1 - zl, c)), (f, tdev(y, zl, 1 - c))
    barrier = pltpu.get_barrier_semaphore()
    for d in (FP, FM, FZ, TP, TM, TZ, TC):
        pl.semaphore_signal(barrier, inc=1, device_id=d, device_id_type=MESH)
    pl.semaphore_wait(barrier, 7)
    n = [0]
    allc = []
    def send(src, dst, dev):
        i = n[0]; n[0] += 1
        cp = pltpu.make_async_remote_copy(src_ref=src, dst_ref=dst, send_sem=ss.at[i], recv_sem=rs.at[i], device_id=dev, device_id_type=MESH)
        cp.start(); allc.append(cp); return cp
    local = []
    def view(o, s):
        return o.at[pl.ds(pl.multiple_of(s * 24, 8), 24)] if len(o.shape) == 2 else o.at[s]
    for i, (s, d) in enumerate(((tok, view(tok_o, t)), (og, view(og_o, t)), (upw, up_o.at[f]), (dww, dw_o.at[f]))):
        cp = pltpu.make_async_copy(s, d, ls.at[i]); cp.start(); local.append(cp)
    got = set()
    def arrive(cp):
        if id(cp) not in got:
            got.add(id(cp)); cp.wait_recv()
    def view(o, s):
        return o.at[pl.ds(pl.multiple_of(s * 24, 8), 24)] if len(o.shape) == 2 else o.at[s]
    W = ((upw, up_o), (dww, dw_o)); A = ((tok, tok_o), (og, og_o))
    fs = lambda x_, z_: fdev(x_, z_)
    ts = lambda y_, z_: tdev(y_, z_, c)
    def first(net, slot, a, z, Pd, Md, Zd):
        h = {}
        for m in (0, 1): h["p", m] = send(net[m][0], view(net[m][1], slot(a, z)), Pd)
        for m in (1, 0): h["m", m] = send(net[m][0], view(net[m][1], slot(a, z)), Md)
        for m in (0, 1): h["z", m] = send(net[m][0], view(net[m][1], slot(a, z)), Zd)
        return h
    def relay_own(h, net, slot, a, ap, am, z, Pd, Md):
        arrive(h["p", 0]); s = slot(am, z); h["dp"] = send(view(net[0][1], s), view(net[0][1], s), Pd)
        arrive(h["m", 1]); s = slot(ap, z); h["dm"] = send(view(net[1][1], s), view(net[1][1], s), Md)
    def cross(h, net, slot, a, z, Pd, Md):
        for m in (0, 1):
            arrive(h["z", m]); s = slot(a, 1 - z)
            h["cp", m] = send(view(net[m][1], s), view(net[m][1], s), Pd)
            h["cm", m] = send(view(net[m][1], s), view(net[m][1], s), Md)
    def relay_oth(h, net, slot, a, ap, am, z, Pd, Md):
        arrive(h["cp", 0]); s = slot(am, 1 - z); h["ep"] = send(view(net[0][1], s), view(net[0][1], s), Pd)
        arrive(h["cm", 1]); s = slot(ap, 1 - z); h["em"] = send(view(net[1][1], s), view(net[1][1], s), Md)
    e = []
    def share(m, s):
        if do_e: e.append(send(view(A[m][1], s), view(A[m][1], s), TC))
    if do_t: ht = first(A, ts, y, zl, TP, TM, TZ)
    if do_f: hf = first(W, fs, x, zh, FP, FM, FZ)
    if do_e:
        for m in (0, 1): e.append(send(A[m][0], view(A[m][1], t), TC))
    if do_t:
        relay_own(ht, A, ts, y, yp, ym, zl, TP, TM)
    if do_f: relay_own(hf, W, fs, x, xp, xm, zh, FP, FM)
    if do_t:
        cross(ht, A, ts, y, zl, TP, TM)
    if do_f: cross(hf, W, fs, x, zh, FP, FM)
    if do_t:
        share(0, ts(ym, zl)); share(1, ts(yp, zl)); share(0, ts(y, 1 - zl)); share(1, ts(y, 1 - zl))
        arrive(ht["p", 1]); share(1, ts(ym, zl)); arrive(ht["m", 0]); share(0, ts(yp, zl))
        relay_oth(ht, A, ts, y, yp, ym, zl, TP, TM)
        share(0, ts(ym, 1 - zl)); share(1, ts(yp, 1 - zl))
    if do_f: relay_oth(hf, W, fs, x, xp, xm, zh, FP, FM)
    if do_t:
        y2 = (y + 2) % 4
        arrive(ht["dp"]); share(0, ts(y2, zl)); arrive(ht["dm"]); share(1, ts(y2, zl))
        arrive(ht["cp", 1]); share(1, ts(ym, 1 - zl)); arrive(ht["cm", 0]); share(0, ts(yp, 1 - zl))
        arrive(ht["ep"]); share(0, ts(y2, 1 - zl)); arrive(ht["em"]); share(1, ts(y2, 1 - zl))
    for cp in allc: arrive(cp)
    for cp in allc: cp.wait_send()
    for cp in local: cp.wait()

def gather_all(tok, og, upw, dww, do_f=True, do_t=True, do_e=True, cid=0):
    bf = jnp.bfloat16
    sh = jax.ShapeDtypeStruct
    return pl.pallas_call(
        functools.partial(gather_kernel, do_f, do_t, do_e),
        out_shape=(sh((384, 8192), bf), sh((384, 8192), bf), sh((8, 16, 128, 128), bf), sh((8, 16, 128, 128), bf)),
        in_specs=[pl.BlockSpec(memory_space=pl.ANY)] * 4,
        out_specs=tuple([pl.BlockSpec(memory_space=pl.ANY)] * 4),
        scratch_shapes=[pltpu.SemaphoreType.DMA((48,)), pltpu.SemaphoreType.DMA((48,)), pltpu.SemaphoreType.DMA((4,))],
        compiler_params=pltpu.CompilerParams(collective_id=cid, has_side_effects=True),
        name="gather_all",
    )(tok, og, upw, dww)


def block_of(ref, b):
    return ref.at[:, pl.ds(pl.multiple_of(b * BLK, BLK), BLK)]

def lanes(tiles):
    return jnp.concatenate([tiles[k, 0] for k in range(8)], axis=1)

def tile_kernel(ui, di, tok, og, wu, wd, mix_o, inp_o, ug_o, dg_o, xs, gs, am, ai):
    j = pl.program_id(0)
    @pl.when(j == 0)
    def _():
        am[...] = jnp.zeros_like(am); ai[...] = jnp.zeros_like(ai)
    for k in range(8):
        xs[:, k * BLK:(k + 1) * BLK] = block_of(tok, ui[j, k])[...]
        gs[:, k * BLK:(k + 1) * BLK] = block_of(og, di[j, k])[...]
    wu2 = wu[...].reshape(1024, BLK)
    wd2 = lanes(wd)
    pre = jnp.dot(xs[...], wu2, preferred_element_type=F32)
    s = 1.0 / (1.0 + jnp.exp(-pre))
    hidden = (pre * s).astype(BF)
    hg = lax.dot_general(gs[...], wd2, (((1,), (1,)), ((), ())), preferred_element_type=F32)
    pg = (hg * s * (1.0 + pre * (1.0 - s))).astype(BF)
    dg = lax.dot_general(hidden, gs[...], (((0,), (0,)), ((), ())), preferred_element_type=F32)
    ug = lax.dot_general(pg, xs[...], (((0,), (0,)), ((), ())), preferred_element_type=F32)
    for k in range(8):
        dg_o[k, 0] = dg[:, k * BLK:(k + 1) * BLK].astype(BF)
        ug_o[k, 0] = ug[:, k * BLK:(k + 1) * BLK].astype(BF)
    out = jnp.dot(hidden, wd2, preferred_element_type=F32)
    for k in range(8):
        r = block_of(am, di[j, k]); r[...] += out[:, k * BLK:(k + 1) * BLK]
    back = lax.dot_general(pg, wu2, (((1,), (1,)), ((), ())), preferred_element_type=F32)
    for k in range(8):
        r = block_of(ai, ui[j, k]); r[...] += back[:, k * BLK:(k + 1) * BLK]
    @pl.when(j == 15)
    def _():
        mix_o[...] = am[...].astype(BF); inp_o[...] = ai[...].astype(BF)

def tiles(ui, di, tok, og, wu, wd):
    sh = jax.ShapeDtypeStruct
    one = pl.Buffered(1)
    whole = pl.BlockSpec((384, 8192), lambda j, *_: (0, 0), pipeline_mode=one)
    part = pl.BlockSpec((8, 1, BLK, BLK), lambda j, *_: (0, j, 0, 0))
    return pl.pallas_call(
        tile_kernel,
        out_shape=(sh((384, 8192), BF), sh((384, 8192), BF), sh((8, 16, BLK, BLK), BF), sh((8, 16, BLK, BLK), BF)),
        grid_spec=pltpu.PrefetchScalarGridSpec(
            num_scalar_prefetch=2, grid=(16,),
            in_specs=[whole, whole, part, part],
            out_specs=(whole, whole, part, part),
            scratch_shapes=[pltpu.VMEM((384, 1024), BF), pltpu.VMEM((384, 1024), BF), pltpu.VMEM((384, 8192), F32), pltpu.VMEM((384, 8192), F32)]),
        compiler_params=pltpu.CompilerParams(vmem_limit_bytes=62 << 20),
        cost_estimate=pl.CostEstimate(flops=10_000_000_000, bytes_accessed=42_000_000, transcendentals=800_000),
        name="tiles",
    )(ui, di, tok, og, wu, wd)


def scatter_kernel(mix, inp, upg, dng, mix_o, inp_o, up_o, dn_o,
                   pf, rf, zf, xf, pt, ct, rt, zt, ss, rs, ls):
    x, zh, y, zl, c = place()
    f, t = fdev(x, zh), tdev(y, zl, c)
    xp, xm, x2 = (x + 1) % 4, (x + 3) % 4, (x + 2) % 4
    yp, ym, y2 = (y + 1) % 4, (y + 3) % 4, (y + 2) % 4
    FP, FM, FZ = (fdev(xp, zh), t), (fdev(xm, zh), t), (fdev(x, 1 - zh), t)
    TP, TM, TZ, TC = (f, tdev(yp, zl, c)), (f, tdev(ym, zl, c)), (f, tdev(y, 1 - zl, c)), (f, tdev(y, zl, 1 - c))
    G = (upg, dng)
    A = (mix, inp)
    nl = [0]; local = {}
    def rows(ref, s):
        return ref.at[pl.ds(pl.multiple_of(s * 24, 8), 24)]
    def load(key, src, dst):
        cp = pltpu.make_async_copy(src, dst, ls.at[nl[0]]); nl[0] += 1
        cp.start(); local[key] = cp
    chips = [(yy, zz) for zz in (0, 1) for yy in (2, 1, 3, 0)]
    def chip(rel):
        dy, own = rel
        return (y + dy) % 4, (zl if own else 1 - zl)
    fk = [(dx, own) for own in (0, 1) for dx in (1, 3, 0)]
    for rel in chips:
        for m in (0, 1):
            yy, zz = chip(rel)
            load(("t", m, rel), rows(A[m], tdev(yy, zz, c)), pt.at[m, rel[1] * 4 + rel[0]])
    for m, dx, own in ((0, 1, 0), (1, 3, 0), (0, 1, 1), (1, 3, 1), (0, 0, 0), (1, 0, 0), (0, 0, 1), (1, 0, 1)):
        load(("f", m, dx, own), G[m].at[fdev((x + dx) % 4, zh if own else 1 - zh)], pf.at[m, own * 2 + (1 if dx else 0)])
    barrier = pltpu.get_barrier_semaphore()
    for d in (FP, FM, FZ, TP, TM, TZ, TC):
        pl.semaphore_signal(barrier, inc=1, device_id=d, device_id_type=MESH)
    pl.semaphore_wait(barrier, 7)
    n = [0]; sent = []
    def send(src, dst, dev):
        i = n[0]; n[0] += 1
        cp = pltpu.make_async_remote_copy(src_ref=src, dst_ref=dst, send_sem=ss.at[i], recv_sem=rs.at[i], device_id=dev, device_id_type=MESH)
        cp.start(); sent.append(cp); return cp
    h = {}
    for rel in chips:
        for m in (0, 1):
            yy, zz = chip(rel)
            h["c", m, rel] = send(rows(A[m], tdev(yy, zz, 1 - c)), ct.at[m, rel[1] * 4 + rel[0]], TC)
    for own in (0, 1):
        zz = zh if own else 1 - zh
        h["ru", own] = send(G[0].at[fdev(x2, zz)], rf.at[0, 0, own], FP)
        h["rd", own] = send(G[1].at[fdev(x2, zz)], rf.at[1, 0, own], FM)
    for own in (0, 1):
        zz = zh if own else 1 - zh
        h["du", own] = send(G[0].at[fdev(xm, zz)], rf.at[0, 1, own], FM)
        h["dd", own] = send(G[1].at[fdev(xp, zz)], rf.at[1, 1, own], FP)

    def add_tiles(dst, a, b, e=None):
        @pl.loop(0, 8)
        def _(i):
            q = pl.ds(i * 2, 2)
            v = a[q].astype(F32) + b[q].astype(F32)
            if e is not None: v = v + e[q].astype(F32)
            dst[q] = v.astype(dst.dtype)
    def add_rows(dst, a, b, e=None):
        @pl.loop(0, 8)
        def _(i):
            q = pl.ds(pl.multiple_of(i * 1024, 1024), 1024)
            v = a[:, q].astype(F32) + b[:, q].astype(F32)
            if e is not None: v = v + e[:, q].astype(F32)
            dst[:, q] = v.astype(dst.dtype)

    def pair(m, rel):
        h["c", m, rel].wait_recv(); local["t", m, rel].wait()
        s = rel[1] * 4 + rel[0]
        add_rows(pt.at[m, s], pt.at[m, s], ct.at[m, s])
    for own in (0, 1):
        pair(0, (2, own)); h["r0", own] = send(pt.at[0, own * 4 + 2], rt.at[0, 0, own], TP)
        pair(1, (2, own)); h["r1", own] = send(pt.at[1, own * 4 + 2], rt.at[1, 0, own], TM)
    for own in (0, 1):
        pair(0, (3, own)); h["d0", own] = send(pt.at[0, own * 4 + 3], rt.at[0, 1, own], TM)
        pair(1, (1, own)); h["d1", own] = send(pt.at[1, own * 4 + 1], rt.at[1, 1, own], TP)
    for own in (0, 1):
        pair(0, (1, own)); pair(1, (3, own))
        h["r0", own].wait_recv(); add_rows(pt.at[0, own * 4 + 1], pt.at[0, own * 4 + 1], rt.at[0, 0, own])
        h["f0", own] = send(pt.at[0, own * 4 + 1], rt.at[0, 2, own], TP)
        h["r1", own].wait_recv(); add_rows(pt.at[1, own * 4 + 3], pt.at[1, own * 4 + 3], rt.at[1, 0, own])
        h["f1", own] = send(pt.at[1, own * 4 + 3], rt.at[1, 2, own], TM)
        local["f", 0, 1, own].wait(); h["ru", own].wait_recv()
        add_tiles(pf.at[0, own * 2 + 1], pf.at[0, own * 2 + 1], rf.at[0, 0, own])
        h["fu", own] = send(pf.at[0, own * 2 + 1], rf.at[0, 2, own], FP)
        local["f", 1, 3, own].wait(); h["rd", own].wait_recv()
        add_tiles(pf.at[1, own * 2 + 1], pf.at[1, own * 2 + 1], rf.at[1, 0, own])
        h["fd", own] = send(pf.at[1, own * 2 + 1], rf.at[1, 2, own], FM)
    for own in (0, 1):
        pair(0, (0, own)); pair(1, (0, own))
        for m in (0, 1):
            h["d%d" % m, own].wait_recv(); h["f%d" % m, own].wait_recv()
            if own == 0:
                add_rows(pt.at[m, 0], pt.at[m, 0], rt.at[m, 1, 0], rt.at[m, 2, 0])
                h["zt", m] = send(pt.at[m, 0], zt.at[m], TZ)
            else:
                h["zt", m].wait_recv()
                add_rows(pt.at[m, 4], pt.at[m, 4], rt.at[m, 1, 1], rt.at[m, 2, 1])
                add_rows((mix_o, inp_o)[m], pt.at[m, 4], zt.at[m])
        for m in (0, 1):
            local["f", m, 0, own].wait()
            h[("du", "dd")[m], own].wait_recv(); h[("fu", "fd")[m], own].wait_recv()
            if own == 0:
                add_tiles(xf.at[m], pf.at[m, 0], rf.at[m, 1, 0], rf.at[m, 2, 0])
                h["zf", m] = send(xf.at[m], zf.at[m], FZ)
            else:
                h["zf", m].wait_recv()
                o = (up_o, dn_o)[m]
                add_tiles(o, pf.at[m, 2], rf.at[m, 1, 1], rf.at[m, 2, 1])
                @pl.loop(0, 8)
                def _(i):
                    q = pl.ds(i * 2, 2)
                    o[q] = o[q] + zf[m, q].astype(F32)
    for cp in sent: cp.wait_send()

def scatter_all(mix, inp, upg, dng, cid=1):
    sh = jax.ShapeDtypeStruct
    V = pltpu.VMEM
    D = 8192
    T = (16, BLK, BLK)
    return pl.pallas_call(
        scatter_kernel,
        out_shape=(sh((24, D), BF), sh((24, D), BF), sh(T, F32), sh(T, F32)),
        in_specs=[pl.BlockSpec(memory_space=pl.ANY)] * 4,
        out_specs=tuple([pl.BlockSpec(memory_space=pltpu.VMEM)] * 4),
        scratch_shapes=[V((2, 4) + T, BF), V((2, 3, 2) + T, BF), V((2,) + T, BF), V((2,) + T, BF),
                        V((2, 8, 24, D), BF), V((2, 8, 24, D), BF), V((2, 3, 2, 24, D), BF), V((2, 24, D), BF),
                        pltpu.SemaphoreType.DMA((48,)), pltpu.SemaphoreType.DMA((48,)), pltpu.SemaphoreType.DMA((32,))],
        compiler_params=pltpu.CompilerParams(collective_id=cid, has_side_effects=True, vmem_limit_bytes=56 << 20),
        name="scatter_all",
    )(mix, inp, upg, dng)


def body(tokens, out_grad, up_weight, down_weight, up_index, down_index):
    T, G, WU, WD = gather_all(tokens, out_grad, up_weight[:, 0], down_weight[:, 0])
    M, I, U, D = tiles(up_index, down_index, T, G, WU, WD)
    mixed, input_grad, up_grad, down_grad = scatter_all(M, I, U, D)
    return mixed, input_grad, up_grad.transpose(0, 2, 1)[:, None], down_grad[:, None]


def solution(mesh):
    rows = P(("fsdp", "tensor"), None)
    tile = P("tensor", "fsdp", None, None)
    index = P("tensor", None)
    return jax.shard_map(
        body,
        mesh=mesh,
        in_specs=(rows, rows, tile, tile, index, index),
        out_specs=(rows, rows, tile, tile),
        check_vma=False,
    )
```

time: 777 us -> 230 us (0.30)
  waiting for transfers between devices: 470 us -> 0 us
  Pallas kernels: 0 us -> 216 us
  matrix products: 154 us -> 0 us
  local copies, waits for them, and re-layouts: 130 us -> 11.1 us
  between operations: 14.4 us -> 0.65 us
    pallas_call x0 -> x3, Pallas kernels: none -> 216 us  [the longest x1 92 us: scatter_all(): pl.pallas_call(scatter_kernel, out_shape=(sh((24, D), BF), sh((24, D), BF...]
    unnamed x8 -> x0, waiting for transfers between devices: 202 us -> none
    dot_general x10 -> x0, matrix products: 154 us -> none  [the longest x2 40.9 us: block_sum(): jnp.einsum('rjko,jkb->rbo', upper, selector, preferred_element_type=jnp.f...]
    reduce_scatter x2 -> x0, waiting for transfers between devices: 145 us -> none  [the longest x1 72.4 us: body(): lax.psum_scatter(block_sum(slot_terms, up_index, block_count).astype(jnp....]
    all_gather x4 -> x0, waiting for transfers between devices: 123 us -> none  [the longest x1 51.4 us: body(): down_full = lax.all_gather(down_weight, 'fsdp', axis=1, tiled=True)]
    gather x4 -> x0, local copies, waits for them, and re-layouts: 54.9 us -> none  [expand(): return jnp.take(blocks, block_index, axis=1)]
    unnamed x12 -> x6, local copies, waits for them, and re-layouts: 40.1 us -> 11.1 us
    all_gather x2 -> x0, local copies, waits for them, and re-layouts: 17.2 us -> none  [the longest x1 8.62 us: body(): grad_rows = lax.all_gather(out_grad, 'tensor', axis=0, tiled=True)]
  transfers between devices with their start and end apart: 7 -> 0, of which waited for: 7 -> 0; matrix products, arithmetic and copies ran while one was open for 33% -> 0% of each run, Pallas kernels for 0% -> 0%
where the time goes in v1:
time: 230 us; the launch traced here: 228 us
  Pallas kernels  216 us (94%)
  local copies, waits for them, and re-layouts  11.1 us (5%)
    pallas_call x1, Pallas kernels, scatter_all(): pl.pallas_call(scatter_kernel, out_shape=(sh((24, D), BF), sh((24, D), BF...  92 us
    pallas_call x1, Pallas kernels, gather_all(): pl.pallas_call(functools.partial(gather_kernel, do_f, do_t, do_e), out_sh...  76.2 us
    pallas_call x1, Pallas kernels, tiles(): pl.pallas_call(tile_kernel, out_shape=(sh((384, 8192), BF), sh((384, 8192...  47.6 us
    unnamed x6, local copies, waits for them, and re-layouts  11.1 us

profile of v1, /device:TPU:0, one launch (start us, length us, event | category | flops | bytes accessed | tf_op | source)
XLA Modules:
  0.0 227.6 jit_solution(2825574253838986421)
XLA Ops:
  0.6 1.4 copy.10.ui
  2.0 1.4 copy.11.di
  3.3 76.2 %gather_all.1 = (bf16[384,8192]{1,0:T(8,128)(2,1)}, bf16[384,8192]{1,0:T(8,128)(2,1)}, bf16[8,16,128,128]{3,2,1,0:T(8,128)(2,1)}, bf16[8,16,128,128]{3,2,1,0:T(8,128)(2,1)}) custom-call(bf16[24,8192]{1,0:T(8,128)(2,1)} %tok.1, bf16[24,8192]{1,0:T(8,128)(2,1)} %og.1, bf16[16,128,128]{2,1,0:T(8,128)(2,1)} %bitcast.10, bf16[16,128,128]{2,1,0:T(8,128)(2,1)} %bitcast.11), custom_call_target="tpu_custom_call" | custom-call | tf_op jit(solution)/shard_map/gather_all/pallas_call | solution.py:101
  79.6 47.6 %tiles.1 = (bf16[384,8192]{1,0:T(8,128)(2,1)}, bf16[384,8192]{1,0:T(8,128)(2,1)}, bf16[8,16,128,128]{3,2,1,0:T(8,128)(2,1)}, bf16[8,16,128,128]{3,2,1,0:T(8,128)(2,1)}) custom-call(s32[16,8]{1,0:T(8,128)} %copy.10.ui, s32[16,8]{1,0:T(8,128)} %copy.11.di, bf16[384,8192]{1,0:T(8,128)(2,1)} %get-tuple-element.16.tok, bf16[384,8192]{1,0:T(8,128)(2,1)} %get-tuple-element.17.og, ...), custom_call_target="tpu_custom_call" | custom-call | flops 10000000000 | bytes 42000000 | tf_op jit(solution)/shard_map/tiles/pallas_call | solution.py:153
  127.2 92.0 %scatter_all.1 = (bf16[24,8192]{1,0:T(8,128)(2,1)}, bf16[24,8192]{1,0:T(8,128)(2,1)}, f32[16,128,128]{2,1,0:T(8,128)}, f32[16,128,128]{2,1,0:T(8,128)}) custom-call(bf16[384,8192]{1,0:T(8,128)(2,1)} %get-tuple-element.20.mix, bf16[384,8192]{1,0:T(8,128)(2,1)} %get-tuple-element.21.inp, bf16[8,16,128,128]{3,2,1,0:T(8,128)(2,1)} %get-tuple-element.22.upg, ...), custom_call_target="tpu_custom_call" | custom-call | tf_op jit(solution)/shard_map/scatter_all/pallas_call | solution.py:286
  219.2 2.5 %copy.12 = f32[16,1,128,128]{3,2,1,0:T(8,128)} copy(f32[16,1,128,128]{2,3,0,1:T(8,128)} %bitcast.9) | data formatting | bytes 2097152
  221.7 1.8 copy.17
  223.5 1.8 copy.18
  225.3 2.3 %copy.19 = f32[16,1,128,128]{3,2,1,0:T(8,128)} copy(f32[16,1,128,128]{3,2,1,0:T(8,128)} %bitcast.8) | data formatting | bytes 2097152

commit v2 on v0

v2 whole, which is shorter than its diff:
```python
import jax
import jax.numpy as jnp
from jax import lax
from jax.experimental import pallas as pl
from jax.experimental.pallas import tpu as pltpu
from jax.sharding import PartitionSpec as P

MESH = pl.DeviceIdType.MESH
F32, BF = jnp.float32, jnp.bfloat16
BLK = 128
D = 8192
NQ = 4
NB = D // BLK
NH = 2


def place():
    f = lax.axis_index("fsdp")
    t = lax.axis_index("tensor")
    return f // 2, f % 2, (t // 2) % 4, t // 8, t % 2


def fdev(x, zh):
    return x * 2 + zh


def tdev(y, zl, c):
    return (zl * 4 + y) * 2 + c


def step_kernel(tok, og, upw, dnw, ui, di, mix_o, inp_o, up_o, dn_o,
                raw, mine, TK, OG, WU, WD, hid, pgs, xs, gs, GP, rf, zf, pt, ct, rt, zt, tabv, tab, ss, rs, ls):
    x, zh, y, zl, c = place()
    f, t = fdev(x, zh), tdev(y, zl, c)
    xp, xm, x2 = (x + 1) % 4, (x + 3) % 4, (x + 2) % 4
    yp, ym, y2 = (y + 1) % 4, (y + 3) % 4, (y + 2) % 4
    FP, FM, FZ = (fdev(xp, zh), t), (fdev(xm, zh), t), (fdev(x, 1 - zh), t)
    TP, TM, TZ, TC = (f, tdev(yp, zl, c)), (f, tdev(ym, zl, c)), (f, tdev(y, 1 - zl, c)), (f, tdev(y, zl, 1 - c))
    JQ = 16 // NQ
    CH = NB // NH
    count = {"r": 0, "l": 0}
    sends = {"a": [], "w": [], "g": []}
    got = set()

    def send(group, src, dst, dev):
        i = count["r"]
        count["r"] += 1
        cp = pltpu.make_async_remote_copy(src_ref=src, dst_ref=dst, send_sem=ss.at[i], recv_sem=rs.at[i],
                                          device_id=dev, device_id_type=MESH)
        cp.start()
        sends[group].append(cp)
        return cp

    def arrive(cp):
        if id(cp) not in got:
            got.add(id(cp))
            cp.wait_recv()

    def local(src, dst):
        i = count["l"]
        count["l"] += 1
        cp = pltpu.make_async_copy(src, dst, ls.at[i])
        cp.start()
        return cp

    def rows(ref, s, col=None):
        r = pl.ds(pl.multiple_of(s * 24, 8), 24)
        return ref.at[:, r] if col is None else ref.at[pl.ds(col * CH, CH), r]

    raws = [local(tok, raw.at[0]), local(og, raw.at[1])]

    lane = lax.broadcasted_iota(jnp.int32, (16, BLK), 1)
    row = lax.broadcasted_iota(jnp.int32, (16, BLK), 0)
    for m, ref in ((0, di), (1, ui)):
        idx = ref[...]
        table = jnp.full((16, BLK), BLK, jnp.int32)
        for k in range(8):
            col = jnp.broadcast_to(idx[:, k:k + 1], (16, BLK))
            table = jnp.where(col == lane, k * 16 + row, table)
            table = jnp.where(lane == 64 + k, col, table)
        tabv[pl.ds(m * 16, 16), :] = table
    table_copy = local(tabv, tab)
    WU[BLK] = jnp.zeros((BLK, BLK), BF)
    WD[BLK] = jnp.zeros((BLK, BLK), BF)
    own = [local(upw, WU.at[pl.ds(f * 16, 16)]), local(dnw, WD.at[pl.ds(f * 16, 16)])]

    barrier = pltpu.get_barrier_semaphore()
    for d in (FP, FM, FZ, TP, TM, TZ, TC):
        pl.semaphore_signal(barrier, inc=1, device_id=d, device_id_type=MESH)
    pl.semaphore_wait(barrier, 7)

    h = {}

    class Net:
        def __init__(self, group, a, ap, am, z, P_, M_, Z_, mine, at):
            self.g, self.a, self.ap, self.am, self.z, self.P, self.M, self.Z = group, a, ap, am, z, P_, M_, Z_
            self.mine, self.at = mine, at

        def key(self, n, q):
            return self.g + n, q

        def out(self, name, m, q, a, z, dev, first=False):
            dst = self.at(m, a, z, q)
            h[self.g, name, m, q] = send(self.g, self.mine(m, q) if first else dst, dst, dev)

        def s1(self, q):
            for name, m, dev in (("p", 0, self.P), ("m", 1, self.M), ("z", 0, self.Z), ("z", 1, self.Z), ("p", 1, self.P), ("m", 0, self.M)):
                self.out(name, m, q, self.a, self.z, dev, True)

        def come(self, name, m, q):
            arrive(h[self.g, name, m, q])

        def s2(self, q):
            self.come("p", 0, q)
            self.out("d", 0, q, self.am, self.z, self.P)
            self.come("m", 1, q)
            self.out("d", 1, q, self.ap, self.z, self.M)
            for m in (0, 1):
                self.come("z", m, q)
                for name, dev in ((("cp", self.P), ("cm", self.M)), (("cm", self.M), ("cp", self.P)))[m]:
                    self.out(name, m, q, self.a, 1 - self.z, dev)

        def s3(self, q):
            self.come("cp", 0, q)
            self.out("e", 0, q, self.am, 1 - self.z, self.P)
            self.come("cm", 1, q)
            self.out("e", 1, q, self.ap, 1 - self.z, self.M)

        def rest(self, q):
            for name, m in (("p", 1), ("m", 0), ("d", 0), ("d", 1), ("cp", 1), ("cm", 0), ("e", 0), ("e", 1)):
                self.come(name, m, q)

    W = (WU, WD)
    A = (TK, OG)
    wn = Net("w", x, xp, xm, zh, FP, FM, FZ,
             lambda m, q: (upw, dnw)[m].at[pl.ds(q * JQ, JQ)],
             lambda m, a, z, q: W[m].at[pl.ds(fdev(a, z) * 16 + q * JQ, JQ)])
    an = Net("a", y, yp, ym, zl, TP, TM, TZ,
             lambda m, q: mine.at[m, pl.ds(q * CH, CH)],
             lambda m, a, z, q: rows(A[m], tdev(a, z, c), q))
    shares = []

    def share(q, *items):
        for m, a, z in items:
            ref = an.at(m, a, z, q)
            shares.append(send("a", ref, ref, TC))

    wn.s1(0)
    for m in (0, 1):
        raws[m].wait()
        for b in range(NB):
            mine[m, b] = raw[m, :, b * BLK:(b + 1) * BLK]
    an.s1(0)
    own += [local(mine.at[m], rows(A[m], t)) for m in (0, 1)]
    wn.s1(1)
    an.s1(1)
    for q in range(NH):
        for m in (0, 1):
            shares.append(send("a", an.mine(m, q), an.at(m, y, zl, q), TC))
    wn.s2(0)
    an.s2(0)
    share(0, (0, ym, zl), (1, yp, zl), (0, y, 1 - zl), (1, y, 1 - zl))
    wn.s1(2)
    wn.s2(1)
    wn.s3(0)
    an.s2(1)
    share(1, (0, ym, zl), (1, yp, zl), (0, y, 1 - zl), (1, y, 1 - zl))
    wn.s1(3)
    an.s3(0)
    share(0, (0, ym, 1 - zl), (1, yp, 1 - zl))
    wn.s2(2)
    wn.s3(1)
    an.s3(1)
    share(1, (0, ym, 1 - zl), (1, yp, 1 - zl))
    wn.s2(3)
    wn.s3(2)
    for q in range(NH):
        an.rest(q)
        share(q, (1, ym, zl), (0, yp, zl), (0, y2, zl), (1, y2, zl), (1, ym, 1 - zl), (0, yp, 1 - zl), (0, y2, 1 - zl), (1, y2, 1 - zl))
    wn.s3(3)
    wn.rest(0)
    for cp in own:
        cp.wait()
    table_copy.wait()
    for cp in shares:
        arrive(cp)

    def products(q):
        @pl.loop(q * JQ, (q + 1) * JQ)
        def _(j):
            for k in range(8):
                xs[:, k * BLK:(k + 1) * BLK] = TK[tab[16 + j, 64 + k]]
                gs[:, k * BLK:(k + 1) * BLK] = OG[tab[j, 64 + k]]
            wu = jnp.concatenate([WU[k * 16 + j] for k in range(8)], axis=0)
            wd = jnp.concatenate([WD[k * 16 + j] for k in range(8)], axis=1)
            pre = jnp.dot(xs[...], wu, preferred_element_type=F32)
            s = 1.0 / (1.0 + jnp.exp(-pre))
            hidden = (pre * s).astype(BF)
            hg = lax.dot_general(gs[...], wd, (((1,), (1,)), ((), ())), preferred_element_type=F32)
            pg = (hg * s * (1.0 + pre * (1.0 - s))).astype(BF)
            at = pl.ds(pl.multiple_of(j * BLK, BLK), BLK)
            hid[:, at] = hidden
            pgs[:, at] = pg
            dg = lax.dot_general(hidden, gs[...], (((0,), (0,)), ((), ())), preferred_element_type=F32)
            ug = lax.dot_general(pg, xs[...], (((0,), (0,)), ((), ())), preferred_element_type=F32)
            for k in range(8):
                GP[0, k, j] = ug[:, k * BLK:(k + 1) * BLK].astype(BF)
                GP[1, k, j] = dg[:, k * BLK:(k + 1) * BLK].astype(BF)

    def gp(m, a, o, q):
        return GP.at[m, fdev(a, zh if o else 1 - zh), pl.ds(q * JQ, JQ)]

    def rfa(m, s, o, q):
        return rf.at[m, s, o, pl.ds(q * JQ, JQ)]

    def f1(q):
        for o in (0, 1):
            h["r", 0, o, q] = send("g", gp(0, x2, o, q), rfa(0, 0, o, q), FP)
            h["r", 1, o, q] = send("g", gp(1, x2, o, q), rfa(1, 0, o, q), FM)
        for o in (0, 1):
            h["x", 0, o, q] = send("g", gp(0, xm, o, q), rfa(0, 1, o, q), FM)
            h["x", 1, o, q] = send("g", gp(1, xp, o, q), rfa(1, 1, o, q), FP)

    def add_tiles(dst, a, b, e=None):
        v = a[...].astype(F32) + b[...].astype(F32)
        if e is not None:
            v = v + e[...].astype(F32)
        dst[...] = v.astype(dst.dtype)

    def f2(q):
        for o in (0, 1):
            for m in (0, 1):
                arrive(h["r", m, o, q])
                part = gp(m, (xp, xm)[m], o, q)
                add_tiles(part, part, rfa(m, 0, o, q))
                h["s", m, o, q] = send("g", part, rfa(m, 2, o, q), (FP, FM)[m])

    def f3(q, o):
        for m in (0, 1):
            arrive(h["x", m, o, q])
            arrive(h["s", m, o, q])
            part = gp(m, x, o, q)
            z = zf.at[m, pl.ds(q * JQ, JQ)]
            if o == 0:
                add_tiles(part, part, rfa(m, 1, o, q), rfa(m, 2, o, q))
                h["zf", m, q] = send("g", part, z, FZ)
            else:
                out = (up_o, dn_o)[m].at[pl.ds(q * JQ, JQ)]
                add_tiles(out, part, rfa(m, 1, o, q), rfa(m, 2, o, q))

    def f4(q):
        for m in (0, 1):
            arrive(h["zf", m, q])
            out = (up_o, dn_o)[m].at[pl.ds(q * JQ, JQ)]
            add_tiles(out, out, zf.at[m, pl.ds(q * JQ, JQ)])

    def dense(m, first, last):
        @pl.loop(first, last)
        def _(i):
            if m == 0:
                w = jnp.concatenate([jnp.concatenate([WD[tab[j, 2 * i + b]] for b in (0, 1)], axis=1) for j in range(16)], axis=0)
                v = jnp.dot(hid[...], w, preferred_element_type=F32)
            else:
                w = jnp.concatenate([jnp.concatenate([WU[tab[16 + j, 2 * i + b]] for j in range(16)], axis=1) for b in (0, 1)], axis=0)
                v = lax.dot_general(pgs[...], w, (((1,), (1,)), ((), ())), preferred_element_type=F32)
            for b in (0, 1):
                A[m][2 * i + b] = v[:, b * BLK:(b + 1) * BLK].astype(BF)

    def chip(m, dy, o, core):
        return rows(A[m], tdev((y + dy) % 4, zl if o else 1 - zl, core))

    order = [(dy, o) for dy in (2, 3, 1, 0) for o in (0, 1)], [(dy, o) for dy in (2, 1, 3, 0) for o in (0, 1)]

    def t0(m):
        for dy, o in order[m]:
            h["c", m, dy, o] = send("g", chip(m, dy, o, 1 - c), ct.at[m, o * 4 + dy], TC)

    loads = {}

    def fetch(m, n):
        if n < 8:
            dy, o = order[m][n]
            loads[m, dy, o] = local(chip(m, dy, o, c), pt.at[m, n % 4]), n % 4

    def t_begin(m):
        t0(m)
        for n in range(4):
            fetch(m, n)

    def add_rows(dst, a, b, e=None):
        @pl.loop(0, 8)
        def _(i):
            q = pl.ds(i * 8, 8)
            v = a[q].astype(F32) + b[q].astype(F32)
            if e is not None:
                v = v + e[q].astype(F32)
            dst[q] = v.astype(dst.dtype)

    def pair(m, dy, o):
        arrive(h["c", m, dy, o])
        cp, slot = loads[m, dy, o]
        cp.wait()
        both = ct.at[m, o * 4 + dy]
        add_rows(both, both, pt.at[m, slot])
        fetch(m, order[m].index((dy, o)) + 4)
        return both

    def t1(m):
        for o in (0, 1):
            h["tr", m, o] = send("g", pair(m, 2, o), rt.at[m, 0, o], (TP, TM)[m])
        for o in (0, 1):
            h["tx", m, o] = send("g", pair(m, (3, 1)[m], o), rt.at[m, 1, o], (TM, TP)[m])

    def t2(m):
        for o in (0, 1):
            both = pair(m, (1, 3)[m], o)
            arrive(h["tr", m, o])
            add_rows(both, both, rt.at[m, 0, o])
            h["ts", m, o] = send("g", both, rt.at[m, 2, o], (TP, TM)[m])

    def t3(m, o):
        both = pair(m, 0, o)
        arrive(h["tx", m, o])
        arrive(h["ts", m, o])
        add_rows(both, both, rt.at[m, 1, o], rt.at[m, 2, o])
        if o == 0:
            h["tz", m] = send("g", both, zt.at[m], TZ)

    def t4(m):
        arrive(h["tz", m])
        for b in range(NB):
            v = ct[m, 4, b].astype(F32) + zt[m, b].astype(F32)
            (mix_o, inp_o)[m][:, b * BLK:(b + 1) * BLK] = v.astype(BF)

    products(0)
    f1(0)
    wn.rest(1)
    products(1)
    f1(1)
    wn.rest(2)
    products(2)
    f1(2)
    wn.rest(3)
    products(3)
    f1(3)
    for cp in sends["a"]:
        cp.wait_send()
    f2(0)
    dense(0, 0, 16)
    f2(1)
    dense(0, 16, 32)
    t_begin(0)
    dense(1, 0, 8)
    t1(0)
    f2(2)
    dense(1, 8, 32)
    t_begin(1)
    t2(0)
    f2(3)
    t1(1)
    f3(0, 0)
    f3(0, 1)
    t3(0, 0)
    f3(1, 0)
    f3(1, 1)
    t2(1)
    f4(0)
    t3(0, 1)
    f3(2, 0)
    f3(2, 1)
    f4(1)
    t4(0)
    f3(3, 0)
    t3(1, 0)
    f3(3, 1)
    t3(1, 1)
    f4(2)
    f4(3)
    t4(1)
    for cp in sends["w"] + sends["g"]:
        cp.wait_send()


def step(tok, og, upw, dnw, ui, di):
    sh = jax.ShapeDtypeStruct
    V = pltpu.VMEM
    T = (16, BLK, BLK)
    R = (NB, 24, BLK)
    hbm = pl.BlockSpec(memory_space=pl.ANY)
    vm = pl.BlockSpec(memory_space=pltpu.VMEM)
    nr = 14 * NQ + 14 * NH + 16 * NH + 14 * NQ + 30
    return pl.pallas_call(
        step_kernel,
        out_shape=(sh((24, D), BF), sh((24, D), BF), sh(T, F32), sh(T, F32)),
        in_specs=[hbm] * 4 + [vm] * 2,
        out_specs=(vm,) * 4,
        scratch_shapes=[V((2, 24, D), BF), V((2,) + R, BF), V((NB, 384, BLK), BF), V((NB, 384, BLK), BF), V((129, BLK, BLK), BF), V((129, BLK, BLK), BF),
                        V((384, 2048), BF), V((384, 2048), BF), V((384, 1024), BF), V((384, 1024), BF),
                        V((2, 8) + T, BF), V((2, 3, 2) + T, BF), V((2,) + T, BF),
                        V((2, 4) + R, BF), V((2, 8) + R, BF), V((2, 3, 2) + R, BF), V((2,) + R, BF),
                        V((32, BLK), jnp.int32), pltpu.SMEM((32, BLK), jnp.int32),
                        pltpu.SemaphoreType.DMA((nr,)), pltpu.SemaphoreType.DMA((nr,)), pltpu.SemaphoreType.DMA((24,))],
        compiler_params=pltpu.CompilerParams(collective_id=0, has_side_effects=True, vmem_limit_bytes=63 << 20),
        name="step",
    )(tok, og, upw, dnw, ui, di)


def body(tokens, out_grad, up_weight, down_weight, up_index, down_index):
    mixed, input_grad, up_grad, down_grad = step(tokens, out_grad, up_weight[:, 0], down_weight[:, 0], up_index, down_index)
    return mixed, input_grad, up_grad.transpose(0, 2, 1)[:, None], down_grad[:, None]


def solution(mesh):
    rows = P(("fsdp", "tensor"), None)
    tile = P("tensor", "fsdp", None, None)
    index = P("tensor", None)
    return jax.shard_map(
        body,
        mesh=mesh,
        in_specs=(rows, rows, tile, tile, index, index),
        out_specs=(rows, rows, tile, tile),
        check_vma=False,
    )
```

time: 777 us -> 185 us (0.24)
  waiting for transfers between devices: 470 us -> 0 us
  Pallas kernels: 0 us -> 177 us
  matrix products: 154 us -> 0 us
  local copies, waits for them, and re-layouts: 130 us -> 7.11 us
  between operations: 14.4 us -> 0.67 us
    unnamed x8 -> x0, waiting for transfers between devices: 202 us -> none
    pallas_call x0 -> x1, Pallas kernels: none -> 177 us  [step(): pl.pallas_call(step_kernel, out_shape=(sh((24, D), BF), sh((24, D), BF),...]
    dot_general x10 -> x0, matrix products: 154 us -> none  [the longest x2 40.9 us: block_sum(): jnp.einsum('rjko,jkb->rbo', upper, selector, preferred_element_type=jnp.f...]
    reduce_scatter x2 -> x0, waiting for transfers between devices: 145 us -> none  [the longest x1 72.4 us: body(): lax.psum_scatter(block_sum(slot_terms, up_index, block_count).astype(jnp....]
    all_gather x4 -> x0, waiting for transfers between devices: 123 us -> none  [the longest x1 51.4 us: body(): down_full = lax.all_gather(down_weight, 'fsdp', axis=1, tiled=True)]
    gather x4 -> x0, local copies, waits for them, and re-layouts: 54.9 us -> none  [expand(): return jnp.take(blocks, block_index, axis=1)]
    unnamed x12 -> x14, local copies, waits for them, and re-layouts: 40.1 us -> 7.11 us
    all_gather x2 -> x0, local copies, waits for them, and re-layouts: 17.2 us -> none  [the longest x1 8.62 us: body(): grad_rows = lax.all_gather(out_grad, 'tensor', axis=0, tiled=True)]
  transfers between devices with their start and end apart: 7 -> 0, of which waited for: 7 -> 0; matrix products, arithmetic and copies ran while one was open for 33% -> 0% of each run, Pallas kernels for 0% -> 0%
where the time goes in v2:
time: 185 us
  Pallas kernels  177 us (96%)
  local copies, waits for them, and re-layouts  7.11 us (4%)
    pallas_call x1, Pallas kernels, step(): pl.pallas_call(step_kernel, out_shape=(sh((24, D), BF), sh((24, D), BF),...  177 us
    unnamed x14, local copies, waits for them, and re-layouts  7.11 us

profile of v2, /device:TPU:0, one launch (start us, length us, event | category | flops | bytes accessed | tf_op | source)
XLA Modules:
  0.0 185.1 jit_solution(4977373276827557698)
XLA Ops:
  0.6 0.0 copy-start.3
  0.6 1.4 copy.10.ui
  2.0 0.0 copy-done.3
  2.0 0.7 copy.11.di
  2.7 177.3 %step.1 = (bf16[24,8192]{1,0:T(8,128)(2,1)}, bf16[24,8192]{1,0:T(8,128)(2,1)}, f32[16,128,128]{2,1,0:T(8,128)}, f32[16,128,128]{2,1,0:T(8,128)}) custom-call(bf16[24,8192]{1,0:T(8,128)(2,1)} %tok.1, bf16[24,8192]{1,0:T(8,128)(2,1)} %og.1, bf16[16,128,128]{2,1,0:T(8,128)(2,1)} %bitcast.10, bf16[16,128,128]{2,1,0:T(8,128)(2,1)} %bitcast.11, s32[16,8]{1,0:T(8,128)} %copy.10.ui, ...), custom_call_target="tpu_custom_call" | custom-call | tf_op jit(solution)/shard_map/step/pallas_call | solution.py:392
  180.0 0.0 copy-start.2
  180.0 0.0 copy-start.1
  180.0 2.6 %copy.12 = f32[16,1,128,128]{3,2,1,0:T(8,128)} copy(f32[16,1,128,128]{2,3,0,1:T(8,128)} %bitcast.9) | data formatting | bytes 2097152
  182.6 0.0 copy-done.2
  182.7 0.0 copy-start
  182.7 0.7 copy.17
  183.4 0.0 copy-done.1
  183.4 0.7 copy.18
  184.1 0.0 copy-done
  184.2 1.0 copy.19
Async XLA Ops:
  0.6 1.4 copy-start.3
  180.0 2.6 %copy-start.2 = (bf16[24,8192]{1,0:T(8,128)(2,1)S(1)}, bf16[24,8192]{1,0:T(8,128)(2,1)}, u32[]{:S(2)}) copy-start(bf16[24,8192]{1,0:T(8,128)(2,1)} %get-tuple-element.20) | copy-start | bytes 1179652
  180.0 3.4 %copy-start.1 = (bf16[24,8192]{1,0:T(8,128)(2,1)S(1)}, bf16[24,8192]{1,0:T(8,128)(2,1)}, u32[]{:S(2)}) copy-start(bf16[24,8192]{1,0:T(8,128)(2,1)} %get-tuple-element.21) | copy-start | bytes 1179652
  182.7 1.5 copy-start
